TPU v7x, 32 devices: a whole 2x2x4 slice. The times are simulated.
32 devices in a mesh: kpt: 4 (over y, core), row: 4 (over z), col: 2 (over x).
Axes of the slice: x: 2, y: 2, z: 4, core: 2. Of those that a mesh axis runs over, the one named last changes fastest.
Arguments:
- a_matrix: bfloat16 [8, 4096, 4096], P('kpt', 'row', 'col'), parts along dimension 0, may hold values from -6 to 6
- b_matrix: bfloat16 [8, 4096, 4096], P('kpt', 'row', 'col'), parts along dimension 0, may hold values from -0.09375 to 0.09375
- a_level: int32 [128, 32], P('kpt'), parts along dimension 0, may hold values from 0 to 4, as said below
- b_level: int32 [128, 32], P('kpt'), parts along dimension 0, may hold values from 0 to 4, as said below
- limit: int32 [128, 32], P(('kpt', 'row'), 'col'), parts along dimension 0, may hold values from 3 to 8
Outputs:
- product: bfloat16 [8, 4096, 4096], P('kpt', 'row', 'col'), parts along dimension 0
- kept_count: int32 [128, 32], P(('kpt', 'row'), 'col'), parts along dimension 0
- kept_total: int32 [4], P('kpt'), parts along dimension 0
There are 4 independent parts, one for each index of `kpt`. A program takes and returns all parts, laid end to end along the dimension named above; each array names one. Nothing has to cross between parts.
Inputs may be any that keep to these rules, and one draw needn't show every extreme that they name: Each block's level is 0 (empty) or its norm exponent 1 to 4; the share of occupied blocks rises from some a sixth in the first block row of a_level (block column of b_level) to some six in seven in the last. `b_level`: as for a_level, with the share rising along block columns.
All inputs are finite; a program needn't handle non-finite values.
Results may differ from a plain program's by a relative error of at most 0.001.
Values may be sent and summed in bfloat16 or wider, within the bound.
No kernel may reach another device: no remote copies, remote signals or barrier semaphores. Data moves between devices by JAX's collectives and lax.ppermute only.
A program may use at most 576 MiB of HBM per device.

v0:
```python
import jax
import jax.numpy as jnp
from jax import lax
from jax.sharding import PartitionSpec as P

BLK = 128


def level_scale(levels):
    power = jnp.power(jnp.float32(2.0), (1 - levels).astype(jnp.float32))
    return jnp.where(levels > 0, power, jnp.float32(0.0))


def spread_blocks(small):
    return jnp.repeat(jnp.repeat(small, BLK, axis=0), BLK, axis=1)


def block_terms(a_piece, a_lev, b_piece, b_lev, limit):
    keep = (
        (a_lev[:, :, None] > 0)
        & (b_lev[None, :, :] > 0)
        & (a_lev[:, :, None] + b_lev[None, :, :] <= limit[:, None, :])
    )
    counted = jnp.sum(keep.astype(jnp.int32), axis=1)
    results = []
    for column in range(limit.shape[1]):
        mask = jnp.repeat(keep[:, :, column], BLK, axis=0)
        masked = jnp.where(mask[None], a_piece, jnp.zeros((), jnp.bfloat16))
        right = b_piece[:, :, column * BLK : (column + 1) * BLK]
        real_real = jnp.dot(masked[0], right[0], preferred_element_type=jnp.float32)
        imag_imag = jnp.dot(masked[1], right[1], preferred_element_type=jnp.float32)
        real_imag = jnp.dot(masked[0], right[1], preferred_element_type=jnp.float32)
        imag_real = jnp.dot(masked[1], right[0], preferred_element_type=jnp.float32)
        results.append(jnp.stack([real_real - imag_imag, real_imag + imag_real]))
    return (jnp.concatenate(results, axis=2), counted)


def shards(a_matrix, b_matrix, a_level, b_level, limit):
    row_place = lax.axis_index("row")
    col_place = lax.axis_index("col")
    row_blocks = a_matrix.shape[1] // BLK
    col_blocks = a_matrix.shape[2] // BLK
    a_own = lax.dynamic_slice(
        a_level, (row_place * row_blocks, col_place * col_blocks), (row_blocks, col_blocks)
    )
    b_own = lax.dynamic_slice(
        b_level, (row_place * row_blocks, col_place * col_blocks), (row_blocks, col_blocks)
    )
    a_eff = a_matrix * spread_blocks(level_scale(a_own)).astype(jnp.bfloat16)[None]
    b_eff = b_matrix * spread_blocks(level_scale(b_own)).astype(jnp.bfloat16)[None]
    a_band = lax.dynamic_slice_in_dim(a_level, row_place * row_blocks, row_blocks, 0)
    b_band = lax.dynamic_slice_in_dim(b_level, col_place * col_blocks, col_blocks, 1)
    a_levels = jnp.repeat(a_band, BLK, axis=1)
    b_levels = jnp.repeat(b_band, BLK, axis=0)
    a_whole = lax.all_gather(a_eff, "col", axis=2, tiled=True)
    added, counted = block_terms(
        a_whole, a_levels, lax.all_gather(b_eff, "row", axis=1, tiled=True), b_levels, limit
    )
    kept_count = counted // BLK
    kept_total = lax.psum(jnp.sum(kept_count).reshape(1), ("row", "col"))
    return (added.astype(jnp.bfloat16), kept_count, kept_total)


def solution(mesh):
    in_specs = (
        P("kpt", "row", "col"),
        P("kpt", "row", "col"),
        P("kpt", None),
        P("kpt", None),
        P(("kpt", "row"), "col"),
    )
    out_specs = (P("kpt", "row", "col"), P(("kpt", "row"), "col"), P("kpt"))
    return jax.shard_map(shards, mesh=mesh, in_specs=in_specs, out_specs=out_specs, check_vma=False)
```

profile of v0, /device:TPU:0, one launch (start us, length us, event | category | flops | bytes accessed | tf_op | source)
XLA Modules:
  0.0 1229.9 jit_solution(12622931891409190300)
XLA Ops:
  25.3 8.4 broadcast_multiply_fusion
  37.7 14.9 %psum.7 = s32[1]{0:T(128)} all-reduce(s32[1]{0:T(128)} %bitcast.131), channel_id=1, replica_groups=mesh['kpt'=4,'row'=4,'col'=2] {'row','col'}, use_global_device_ids=true, to_apply=%region_2.3 | all-reduce | flops 1 | bytes 8 | tf_op jit(solution)/shard_map/psum | solution.py:60
  52.6 167.8 %all-gather.3.cloned.1.call-done = bf16[2,1024,4096]{2,1,0:T(8,128)(2,1)} async-done(((bf16[2,1024,2048]{2,1,0:T(8,128)(2,1)}), bf16[2,1024,4096]{2,1,0:T(8,128)(2,1)}) %all-gather.3.cloned.1.call-update) | async-done | bytes 16777232 | tf_op jit(solution)/shard_map/all_gather | solution.py:55
  285.2 115.2 %broadcast_select_fusion = (bf16[2,1024,4096]{2,1,0:T(8,128)(2,1)}, bf16[2,1024,4096]{2,1,0:T(8,128)(2,1)}, bf16[2,1024,4096]{2,1,0:T(8,128)(2,1)}, bf16[2,1024,...) fusion(bf16[2,1024,4096]{2,1,0:T(8,128)(2,1)} %all-gather.3.clo, ...), kind=kLoop, calls=%fused_computation | loop fusion | flops 134217728 | bytes 352321536 | tf_op jit(solution)/shard_map/jit(_where)/select_n | solution.py:28
  400.4 383.0 %all-gather.5.cloned.1.call-done = bf16[2,4096,2048]{2,1,0:T(8,128)(2,1)} async-done(((bf16[2,1024,2048]{2,1,0:T(8,128)(2,1)}), bf16[2,4096,2048]{2,1,0:T(8,128)(2,1)}) %all-gather.5.cloned.1.call-update) | async-done | bytes 33554448 | tf_op jit(solution)/shard_map/all_gather | solution.py:57
  783.4 6.7 fusion.1
  811.6 6.5 fusion.4
  818.1 6.9 fusion.157
  838.9 6.5 fusion.8
  845.4 6.5 fusion.155
  859.3 6.7 fusion.13
  865.9 6.5 fusion.12
  872.5 6.5 fusion.153
  892.8 6.5 fusion.16
  899.4 6.7 fusion.151
  919.9 6.5 fusion.20
  926.5 6.5 fusion.149
  940.3 6.9 fusion.25
  947.2 6.5 fusion.24
  953.7 6.5 fusion.147
  974.1 6.5 fusion.28
  980.6 6.7 fusion.145
  1021.5 6.7 fusion.37
  1055.1 6.5 fusion.40
  1061.7 6.9 fusion.139
  1082.4 6.5 fusion.44
  1102.8 6.7 fusion.49
  1136.4 6.5 fusion.52
  1142.9 6.7 fusion.133
  1163.4 6.5 fusion.56
  1190.3 6.8 fusion.60
  1211.0 11.6 copy.28
  (104 shorter events, 342.0 us)
Async XLA Ops:
  7.2 213.3 %all-gather.3.cloned.1.call-start = ((), (), s32[]{:S(2)}) async-start(), calls=%async_computation | async-start | bytes 25165824 | tf_op jit(solution)/shard_map/all_gather | solution.py:55
  7.2 7.6 copy-start.1
  18.6 764.8 %all-gather.5.cloned.1.call-start = ((), (), s32[]{:S(2)}) async-start(), calls=%async_computation.1 | async-start | bytes 41943040 | tf_op jit(solution)/shard_map/all_gather | solution.py:57
  25.3 8.4 copy-start.2
  25.3 9.6 copy-start.3
  783.4 8.5 copy-start
Sparse Core Ops, SparseCore 0:
  18.7 201.6 all-gather.2
  222.0 561.3 all-gather.4
where the time goes:
time: 1240 us; the launch traced here: 1230 us
  waiting for transfers between devices  551 us (44%)
  matrix products  412 us (33%)
  other arithmetic  144 us (12%)
  local copies, waits for them, and re-layouts  92.9 us (7%)
  between operations  15.1 us (1%)
  blocking collectives  14.9 us (1%)
    all_gather x1, waiting for transfers between devices, shards(): lax.all_gather(b_eff, 'row', axis=1, tiled=True)  383 us
    all_gather x1, waiting for transfers between devices, shards(): a_whole = lax.all_gather(a_eff, 'col', axis=2, tiled=True)  168 us
    select_n x1, other arithmetic, block_terms(): masked = jnp.where(mask[None], a_piece, jnp.zeros((), jnp.bfloat16))  115 us
    dot_general x16, matrix products, block_terms(): real_real = jnp.dot(masked[0], right[0], preferred_element_type=jnp.float32)  105 us
    dot_general x16, matrix products, block_terms(): imag_imag = jnp.dot(masked[1], right[1], preferred_element_type=jnp.float32)  103 us
    dot_general x16, matrix products, block_terms(): real_imag = jnp.dot(masked[0], right[1], preferred_element_type=jnp.float32)  102 us
    dot_general x16, matrix products, block_terms(): imag_real = jnp.dot(masked[1], right[0], preferred_element_type=jnp.float32)  102 us
    broadcast_in_dim x16, local copies, waits for them, and re-layouts, block_terms(): mask = jnp.repeat(keep[:, :, column], BLK, axis=0)  64.7 us
  transfers between devices with their start and end apart: 2, of which 2 were waited for; matrix products, arithmetic and copies ran while one was open for 16% of the time, Pallas kernels for 0%

commit v1 on v0

v1 whole, which is shorter than its diff:
```python
import functools

import jax
import jax.numpy as jnp
from jax import lax
from jax.experimental import pallas as pl
from jax.experimental.pallas import tpu as pltpu
from jax.sharding import PartitionSpec as P


BLK = 128
GROUP = 4
ANY = pl.BlockSpec(memory_space=pl.ANY)
SMEM = pl.BlockSpec(memory_space=pltpu.SMEM)


def level_scale(levels):
    power = jnp.power(jnp.float32(2.0), (1 - levels).astype(jnp.float32))
    return jnp.where(levels > 0, power, jnp.float32(0.0))


def as_real(block):
    real, imag = block[0], block[1]
    return jnp.concatenate(
        [jnp.concatenate([real, imag], 1), jnp.concatenate([-imag, real], 1)], 0
    )


def add_block(acc, left, block, scales, base, row_blocks):
    added = jnp.dot(left[...], as_real(block), preferred_element_type=jnp.float32)
    for i in range(row_blocks):
        rows = pl.ds(i * BLK, BLK)
        acc[rows, :] += added[i * BLK : (i + 1) * BLK] * scales[base + i]


def pair_copies(source, column, target, sem):
    return [
        pltpu.make_async_copy(
            source.at[part, :, pl.ds(column, BLK)],
            target.at[:, pl.ds(part * BLK, BLK)],
            sem.at[part],
        )
        for part in range(2)
    ]


def dense_kernel(row_blocks, k_blocks, scales, wanted, a_ref, b_ref, out_ref, left, acc, sem):
    j = pl.program_id(0)

    @pl.when(j == 0)
    def _():
        for k in range(k_blocks):
            for copy in pair_copies(a_ref, k * BLK, left.at[k], sem.at[k]):
                copy.start()
        for k in range(k_blocks):
            for copy in pair_copies(a_ref, k * BLK, left.at[k], sem.at[k]):
                copy.wait()

    acc[...] = jnp.zeros_like(acc)

    @pl.loop(0, k_blocks)
    def _(k):
        at = j * k_blocks + k

        @pl.when(wanted[at] > 0)
        def _():
            block = b_ref.at[:, pl.ds(pl.multiple_of(k * BLK, BLK), BLK), :]
            add_block(acc, left.at[k], block[...], scales, at * row_blocks, row_blocks)

    out_ref[0] = acc[:, :BLK].astype(out_ref.dtype)
    out_ref[1] = acc[:, BLK:].astype(out_ref.dtype)


def dense_product(a_whole, b_whole, scale):
    cols, k_blocks, row_blocks = scale.shape
    rows = row_blocks * BLK
    wanted = jnp.any(scale > 0, axis=2).astype(jnp.int32).reshape(-1)
    return pl.pallas_call(
        functools.partial(dense_kernel, row_blocks, k_blocks),
        out_shape=jax.ShapeDtypeStruct((2, rows, cols * BLK), jnp.bfloat16),
        grid=(cols,),
        in_specs=[SMEM, SMEM, ANY, pl.BlockSpec((2, k_blocks * BLK, BLK), lambda j: (0, 0, j))],
        out_specs=pl.BlockSpec((2, rows, BLK), lambda j: (0, 0, j)),
        scratch_shapes=[
            pltpu.VMEM((k_blocks, rows, 2 * BLK), jnp.bfloat16),
            pltpu.VMEM((rows, 2 * BLK), jnp.float32),
            pltpu.SemaphoreType.DMA((k_blocks, 2)),
        ],
        name="dense",
    )(scale.reshape(-1), wanted, a_whole, b_whole)


def pack_kernel(low, lead, row_blocks, with_given, shifted, *refs):
    listed, facts, own = refs[:3]
    given = refs[3] if with_given else None
    out_ref, sem = refs[-2:]
    moved, shift = facts[0], facts[1] * shifted

    def own_copy(q, slot):
        row = pl.multiple_of(lax.rem(slot, row_blocks) * BLK, BLK)
        column = pl.multiple_of(lax.div(slot, row_blocks) * BLK, BLK)
        window = own.at[:, pl.ds(row, BLK), pl.ds(column, BLK)]
        return pltpu.make_async_copy(window, out_ref.at[q], sem.at[q])

    @pl.loop(0, out_ref.shape[0])
    def _(q):
        place = q + low
        if with_given:
            among = (place >= lead) & (place < lead + moved)
            rank = jnp.where(place >= lead, place - moved, place)

            @pl.when(among)
            def _():
                one = given.at[jnp.clip(place - lead, 0, given.shape[0] - 1)]
                pltpu.make_async_copy(one, out_ref.at[q], sem.at[q]).start()

            @pl.when(jnp.logical_not(among))
            def _():
                own_copy(q, listed[jnp.clip(rank, 0, listed.shape[0] - 1)]).start()

        else:
            own_copy(q, listed[jnp.clip(place + shift, 0, listed.shape[0] - 1)]).start()

    @pl.loop(0, out_ref.shape[0])
    def _(q):
        own_copy(q, 0).wait()


def pack(listed, facts, own, given, low, count, lead, row_blocks, shifted):
    operands = [listed, facts, own] + ([] if given is None else [given])
    return pl.pallas_call(
        functools.partial(pack_kernel, low, lead, row_blocks, given is not None, shifted),
        out_shape=jax.ShapeDtypeStruct((count, 2, BLK, BLK), own.dtype),
        in_specs=[SMEM, SMEM] + [ANY] * (len(operands) - 2),
        out_specs=pl.BlockSpec(memory_space=pltpu.VMEM),
        scratch_shapes=[pltpu.SemaphoreType.DMA((count,))],
        cost_estimate=pl.CostEstimate(
            flops=0, transcendentals=0, bytes_accessed=count * 8 * BLK * BLK
        ),
        name="pack",
    )(*operands)


def pick_kernel(ranges, here, *refs):
    out_ref, sem = refs[-2:]
    for act in ("start", "wait"):
        for (low, high), ref in zip(ranges, refs):

            @pl.when((here[0] >= low) & (here[0] <= high))
            def _():
                getattr(pltpu.make_async_copy(ref, out_ref, sem), act)()


def pick(here, ranges, arrays):
    shape = arrays[0].shape
    return pl.pallas_call(
        functools.partial(pick_kernel, ranges),
        out_shape=jax.ShapeDtypeStruct(shape, arrays[0].dtype),
        in_specs=[SMEM] + [ANY] * len(arrays),
        out_specs=pl.BlockSpec(memory_space=pltpu.VMEM),
        scratch_shapes=[pltpu.SemaphoreType.DMA],
        cost_estimate=pl.CostEstimate(
            flops=0, transcendentals=0, bytes_accessed=shape[0] * 8 * BLK * BLK
        ),
        name="pick",
    )(here, *arrays)


def phase_kernel(plan, ranges, with_part, final, *refs):
    slots, row_blocks, sizes = plan
    refs = list(refs)
    take = lambda n: [refs.pop(0) for _ in range(n)]
    facts, starts, lefts, rights, bases, scales = take(6)
    factors = take(3)
    lists = []
    for t in slots:
        choices = [take(len(sizes) - 1) for _ in ranges[t]]
        lists.append((choices, take(1)[0]))
    part_ref = take(1)[0] if with_part else None
    out_ref, left, held, acc, a_sem, b_sem = refs
    j = pl.program_id(0)
    here = facts[0]

    def left_copies(act):
        for n, t in enumerate(slots):
            for which, ref in enumerate(factors):

                @pl.when(facts[1 + 2 * t] == which)
                def _():
                    @pl.loop(0, row_blocks)
                    def _(kk):
                        column = pl.multiple_of((facts[2 + 2 * t] + kk) * BLK, BLK)
                        at = n * row_blocks + kk
                        for copy in pair_copies(ref, column, left.at[at], a_sem.at[at]):
                            act(copy)

    def held_copies(act):
        for n, t in enumerate(slots):
            choices, hop = lists[n]
            at = n * sum(sizes)
            for (low, high), arrays in zip(ranges[t], choices):

                @pl.when((here >= low) & (here <= high))
                def _():
                    for m, array in enumerate(arrays):
                        target = held.at[pl.ds(at + sum(sizes[:m]), sizes[m])]
                        act(pltpu.make_async_copy(array, target, b_sem.at[n, m]))

            m = len(sizes) - 1
            target = held.at[pl.ds(at + sum(sizes[:m]), sizes[m])]
            act(pltpu.make_async_copy(hop, target, b_sem.at[n, m]))

    @pl.when(j == 0)
    def _():
        left_copies(lambda copy: copy.start())
        held_copies(lambda copy: copy.start())
        left_copies(lambda copy: copy.wait())
        held_copies(lambda copy: copy.wait())

    acc[...] = part_ref[0] if with_part else jnp.zeros_like(acc)

    @pl.loop(starts[j], starts[j + 1])
    def _(group):
        entries = [group * GROUP + q for q in range(GROUP)]
        right = jnp.concatenate([as_real(held[rights[e]]) for e in entries], 0)
        scaled = []
        for e in entries:
            factor, base = left[lefts[e]], bases[e]
            rows = [
                factor[i * BLK : (i + 1) * BLK] * scales[base + i].astype(factor.dtype)
                for i in range(row_blocks)
            ]
            scaled.append(jnp.concatenate(rows, 0))
        whole = jnp.concatenate(scaled, 1)
        acc[...] += jnp.dot(whole, right, preferred_element_type=jnp.float32)

    if final:
        out_ref[0] = acc[:, :BLK].astype(out_ref.dtype)
        out_ref[1] = acc[:, BLK:].astype(out_ref.dtype)
    else:
        out_ref[0] = acc[...]


def phase(slots, facts, entries, scales, factors, segments, sizes, ranges, part, final):
    _, rows, width = factors[0].shape
    row_blocks = rows // BLK
    cols = width // BLK
    operands = [facts, *entries, scales] + list(factors)
    loaded = len(operands) - len(factors)
    for t in slots:
        choices, hop = segments[t]
        for arrays in choices:
            operands += arrays
        operands.append(hop)
    specs = [SMEM] * loaded + [ANY] * (len(operands) - loaded)
    if part is not None:
        operands.append(part)
        specs.append(pl.BlockSpec((1, rows, 2 * BLK), lambda j: (j, 0, 0)))
    if final:
        out_shape = jax.ShapeDtypeStruct((2, rows, cols * BLK), factors[0].dtype)
        out_spec = pl.BlockSpec((2, rows, BLK), lambda j: (0, 0, j))
    else:
        out_shape = jax.ShapeDtypeStruct((cols, rows, 2 * BLK), jnp.float32)
        out_spec = pl.BlockSpec((1, rows, 2 * BLK), lambda j: (j, 0, 0))
    plan = (slots, row_blocks, sizes)
    return pl.pallas_call(
        functools.partial(phase_kernel, plan, ranges, part is not None, final),
        out_shape=out_shape,
        grid=(cols,),
        in_specs=specs,
        out_specs=out_spec,
        scratch_shapes=[
            pltpu.VMEM((len(slots) * row_blocks, rows, 2 * BLK), factors[0].dtype),
            pltpu.VMEM((len(slots) * sum(sizes), 2, BLK, BLK), factors[0].dtype),
            pltpu.VMEM((rows, 2 * BLK), jnp.float32),
            pltpu.SemaphoreType.DMA((len(slots) * row_blocks, 2)),
            pltpu.SemaphoreType.DMA((len(slots), len(sizes))),
        ],
        cost_estimate=pl.CostEstimate(
            flops=4 * len(slots) * rows * rows * cols * BLK,
            transcendentals=0,
            bytes_accessed=64 * rows * rows,
        ),
        name="phase",
    )(*operands)


def ranks(flags):
    size = flags.shape[-1]
    before = jnp.arange(size)[:, None] < jnp.arange(size)[None, :]
    set_before = jnp.sum(flags[..., :, None] & before, axis=-2, dtype=jnp.int32)
    return set_before, jnp.sum(flags, axis=-1, dtype=jnp.int32)


def compacted(flags, rank, values):
    hit = flags[..., None, :] & (rank[..., None, :] == jnp.arange(flags.shape[-1])[:, None])
    return jnp.sum(jnp.where(hit, values[..., None, :], 0), axis=-1, dtype=jnp.int32)


def entry_lists(flags, lefts, rights, bases, nothing):
    cols, among = flags.shape
    within, counts = ranks(flags)
    groups = (counts + GROUP - 1) // GROUP
    first = jnp.arange(cols)[:, None] > jnp.arange(cols)[None, :]
    starts = jnp.sum(first * groups[None, :], axis=1, dtype=jnp.int32)
    room = cols * among
    spot = (GROUP * starts[:, None] + within).reshape(-1)
    hit = flags.reshape(-1)[None] & (spot[None] == jnp.arange(room)[:, None])
    listed = lambda values, empty: empty + jnp.sum(
        jnp.where(hit, values.reshape(-1)[None] - empty, 0), axis=1, dtype=jnp.int32
    )
    starts = jnp.concatenate([starts, jnp.sum(groups, dtype=jnp.int32)[None]])
    return starts, listed(lefts, 0), listed(rights, 0), listed(bases, nothing)


def ring(nrow, step):
    return [(i, (i + step) % nrow) for i in range(nrow)]


def listed_product(a_matrix, b_matrix, b_level, scale, nrow, kept):
    row = lax.axis_index("row")
    col = lax.axis_index("col")
    cols, _, row_blocks = scale.shape
    wide = cols * row_blocks
    lead = 5 * wide // 16
    spare = 7 * wide // 32
    rest = wide // 16
    sizes = (lead, spare, rest, spare)
    room = lead + spare + rest

    by_place = b_level.reshape(nrow, row_blocks, 2, cols).transpose(2, 0, 3, 1) > 0
    occupied = by_place.reshape(2, nrow, wide)
    rank, counts = ranks(occupied)
    moved = jnp.clip((counts[1] - counts[0]) // 2, 0, spare)
    light = jnp.where(moved > 0, jnp.maximum(counts[0], lead) + moved, counts[0])
    heavy = counts[1] - moved
    too_long = jnp.any((light > room) | (heavy > room))

    ranges = {t: [(t, nrow - 1)] + [(r, r) for r in range(t)] for t in range(nrow)}

    own_rank = lax.dynamic_slice(rank, (col, row, 0), (1, 1, wide))[0, 0]
    own_set = lax.dynamic_slice(occupied, (col, row, 0), (1, 1, wide))[0, 0]
    listed = compacted(own_set, own_rank, jnp.arange(wide))
    zero = jnp.zeros((), jnp.int32)
    pack_facts = jnp.stack([jnp.where(col == 0, moved[row], zero), heavy[row]])
    packed = functools.partial(pack, listed, pack_facts, b_matrix)

    steps = jnp.arange(nrow)
    source = jnp.where(steps <= row, row - steps, steps)
    rank_here = rank[col][source]
    moved_here = moved[source][:, None]
    heavy_here = heavy[source][:, None]
    first_side = jnp.where(rank_here < lead, rank_here, rank_here + moved_here)
    last_side = jnp.where(rank_here < heavy_here, rank_here, room + rank_here - heavy_here)
    place = jnp.where(col == 0, first_side, last_side).reshape(nrow, cols, row_blocks)
    by_source = scale.reshape(cols, nrow, row_blocks, row_blocks)[:, source].transpose(1, 0, 2, 3)
    wanted = jnp.any(by_source > 0, axis=3)
    nothing = nrow * wide * row_blocks
    scales = jnp.concatenate([by_source.reshape(-1), jnp.zeros((row_blocks,), jnp.float32)])
    bases = (jnp.arange(nrow * wide) * row_blocks).reshape(nrow, cols, row_blocks)
    start = source * row_blocks
    which = jnp.where(start // cols == col, 0, jnp.where(col == 1, 1, 2))
    facts = jnp.concatenate([row[None], jnp.stack([which, start % cols], 1).reshape(-1)])
    facts = facts.astype(jnp.int32)
    held_room = sum(sizes)

    def entries_of(slots):
        at = jnp.array(slots)
        among = jnp.arange(len(slots))[:, None, None]
        across = lambda x: x.transpose(1, 0, 2).reshape(cols, -1)
        lefts = jnp.broadcast_to(among * row_blocks + jnp.arange(row_blocks), place[at].shape)
        rights = jnp.clip(place, 0, held_room - 1)[at] + among * held_room
        return entry_lists(
            across(wanted[at]), across(lefts), across(rights), across(bases[at]), nothing
        )

    plans = [(0, 1)] + [(t,) for t in range(2, nrow)]
    lists = [entries_of(slots) for slots in plans]

    def chunk(given, low, size, shifted=0):
        return packed(given, low, size, lead, row_blocks, shifted)

    def move(array, axis, pairs):
        return lax.ppermute(array, axis, pairs)

    def forward(t, m):
        rises = [(i, i + 1) for i in range(t - 1, nrow - 1)]
        falls = [(i + 1, i) for i in range(nrow - t)]
        up[t][m] = move(up[t - 1][m], "row", rises)
        down[t][m] = move(down[t - 1][m], "row", falls)

    up = [[None] * 3 for _ in range(nrow)]
    down = [[None] * 3 for _ in range(nrow)]
    hops = [None] * nrow

    def hop(t):
        choices = [up[t][1]] + [down[t - r][1] for r in range(t)]
        chosen = pick(row[None].astype(jnp.int32), ranges[t], choices)
        if t == nrow - 2:
            nonlocal facts, scales, lists
            held = (chosen, facts, scales, lists)
            chosen, facts, scales, lists = lax.optimization_barrier(held)
        hops[t] = move(chosen, "col", [(0, 1)])

    a_first = move(a_matrix, "col", [(0, 1)])
    up[0][0] = down[0][0] = chunk(None, 0, lead)
    forward(1, 0)
    hops[0] = chunk(None, 0, spare, 1)
    given = move(hops[0], "col", [(1, 0)])
    up[0][1] = down[0][1] = chunk(given, lead, spare)
    forward(1, 1)
    a_last = move(a_matrix, "col", [(1, 0)])
    up[0][2] = down[0][2] = chunk(given, lead + spare, rest)
    forward(1, 2)
    pair_sum = kept + move(kept, "col", [(0, 1), (1, 0)])
    hop(1)
    for t in range(2, nrow):
        for m in (1, 0, 2):
            forward(t, m)
            if m == 1 and t < nrow - 1:
                hop(t)
        if t == 2:
            kept_total = pair_sum
            for step in range(1, nrow):
                kept_total += move(pair_sum, "row", ring(nrow, step))

    def add(n, part, final):
        slots = plans[n]
        segments = {t: ([up[t]] + [down[t - r] for r in range(t)], hops[t]) for t in slots}
        return phase(slots, facts, lists[n], scales, factors, segments, sizes, ranges, part, final)

    far = nrow - 1
    factors = (a_matrix, a_first, a_last)
    part = add(0, None, False)
    hop(far)
    for n in range(1, len(plans) - 1):
        part = add(n, part, False)

    def all_blocks():
        pieces = [b_matrix]
        for _ in range(1, nrow):
            pieces.append(lax.ppermute(pieces[-1], "row", ring(nrow, 1)))
        b_whole = jnp.stack(pieces)[(row - steps) % nrow].transpose(1, 0, 2, 3)
        b_whole = b_whole.reshape(2, -1, b_matrix.shape[2])
        a_whole = jnp.where(
            col == 0,
            jnp.concatenate([a_matrix, a_last], 2),
            jnp.concatenate([a_first, a_matrix], 2),
        )
        return dense_product(a_whole, b_whole, scale)

    def listed_blocks():
        return add(len(plans) - 1, part, True)

    return lax.cond(too_long, all_blocks, listed_blocks), kept_total


def shards(nrow, in_pairs, a_matrix, b_matrix, a_level, b_level, limit):
    row = lax.axis_index("row")
    col = lax.axis_index("col")
    row_blocks, cols = limit.shape
    a_here = lax.dynamic_slice_in_dim(a_level, row * row_blocks, row_blocks, 0)
    b_here = lax.dynamic_slice_in_dim(b_level, col * cols, cols, 1)
    left = a_here.T[None]
    right = b_here.T[:, :, None]
    keep = (left > 0) & (right > 0) & (left + right <= limit.T[:, None, :])
    kept_count = jnp.sum(keep, axis=1, dtype=jnp.int32).T
    kept = jnp.sum(kept_count).reshape(1)
    scale = jnp.where(keep, level_scale(left) * level_scale(right), jnp.float32(0.0))
    if in_pairs:
        product, kept_total = listed_product(a_matrix, b_matrix, b_level, scale, nrow, kept)
    else:
        a_whole = lax.all_gather(a_matrix, "col", axis=2, tiled=True)
        b_whole = lax.all_gather(b_matrix, "row", axis=1, tiled=True)
        product = dense_product(a_whole, b_whole, scale)
        kept_total = lax.psum(kept, ("row", "col"))
    return (product, kept_count, kept_total)


def solution(mesh):
    in_specs = (
        P("kpt", "row", "col"),
        P("kpt", "row", "col"),
        P("kpt", None),
        P("kpt", None),
        P(("kpt", "row"), "col"),
    )
    out_specs = (P("kpt", "row", "col"), P(("kpt", "row"), "col"), P("kpt"))
    nrow, ncol = mesh.shape["row"], mesh.shape["col"]
    in_pairs = ncol == 2 and nrow > 2

    def body(*args):
        return shards(nrow, in_pairs, *args)

    return jax.shard_map(body, mesh=mesh, in_specs=in_specs, out_specs=out_specs, check_vma=False)
```

time: 1240 us -> 574 us (0.46)
  the two profiles are of different devices: /device:TPU:0 before, /device:TPU:10 now
where the time goes in v1:
time: 574 us; the launch traced here: 572 us
  waiting for transfers between devices  328 us (57%)
  Pallas kernels  130 us (23%)
  starting transfers between devices  82.5 us (14%)
  other arithmetic  14.8 us (3%)
  local copies, waits for them, and re-layouts  10.1 us (2%)
  between operations  7.07 us (1%)
    ppermute x28, waiting for transfers between devices, move(): return lax.ppermute(array, axis, pairs)  328 us
    pallas_call x3, Pallas kernels, phase(): pl.pallas_call(functools.partial(phase_kernel, plan, ranges, part is not...  107 us
    ppermute x28, starting transfers between devices, move(): return lax.ppermute(array, axis, pairs)  82.5 us
    pallas_call x4, Pallas kernels, pack(): pl.pallas_call(functools.partial(pack_kernel, low, lead, row_blocks, give...  15.5 us
  transfers between devices with their start and end apart: 28, of which 11 were waited for; matrix products, arithmetic and copies ran while one was open for 3% of the time, Pallas kernels for 17%

profile of v1, /device:TPU:10, one launch (start us, length us, event | category | flops | bytes accessed | tf_op | source)
XLA Modules:
  0.0 572.2 jit_solution(7370399097992835642)
XLA Ops:
  6.9 4.5 pack.4.refs_12_
  11.4 4.0 collective-permute-start.3
  15.4 4.4 pack.6.refs_9_
  21.8 3.9 collective-permute-start.10
  28.4 5.9 %collective-permute-start.27 = (s32[1]{0:T(128)}, s32[1]{0:T(128)}, u32[]{:S(2)}, u32[]{:S(2)}) collective-permute-start(s32[1]{0:T(128)} %bitcast.34), channel_id=1, source_target_pairs={{0,1},{1,0},{2,3},{3,2},{4,5},{5,4},{6,7},{7,6},{8,9},{9,8},{10,11... | collective-permute-start | bytes 20 | tf_op jit(solution)/shard_map/ppermute | solution.py:384
  34.3 175.0 %collective-permute-done.27 = s32[1]{0:T(128)} collective-permute-done((s32[1]{0:T(128)}, s32[1]{0:T(128)}, u32[]{:S(2)}, u32[]{:S(2)}) %collective-permute-start.27) | collective-permute-done | bytes 36 | tf_op jit(solution)/shard_map/ppermute | solution.py:384
  209.3 4.6 collective-permute-start.9
  215.3 4.4 collective-permute-start.28
  219.7 2.7 pack.7.refs_11_
  232.4 9.2 %collective-permute-done.14.refs_15_ = bf16[8,2,128,128]{3,2,1,0:T(8,128)(2,1)S(1)} collective-permute-done((bf16[8,2,128,128]{3,2,1,0:T(8,128)(2,1)}, bf16[8,2,128,128]{3,2,1,0:T(8,128)(2,1)S(1)}, u32[]{:S(2)}, u32[]{:S(2)}) %collective-permute-start.14) | collective-permute-done | bytes 524320 | tf_op jit(solution)/shard_map/ppermute | solution.py:384
  244.6 3.8 pack.5.refs_10_
  248.4 4.5 collective-permute-done.21.refs_18_.refs_17_
  252.9 3.1 collective-permute-start.4
  257.2 4.1 collective-permute-start.18
  261.4 3.3 collective-permute-start.15
  265.4 34.8 %collective-permute-done.15.refs_11_ = bf16[8,2,128,128]{3,2,1,0:T(8,128)(2,1)S(1)} collective-permute-done((bf16[8,2,128,128]{3,2,1,0:T(8,128)(2,1)S(1)}, bf16[8,2,128,128]{3,2,1,0:T(8,128)(2,1)S(1)}, u32[]{:S(2)}, u32[]{:S(2)}) %collective-permute-start.15) | collective-permute-done | bytes 524320 | tf_op jit(solution)/shard_map/ppermute | solution.py:384
  304.5 5.9 %collective-permute-start.11 = (bf16[40,2,128,128]{3,2,1,0:T(8,128)(2,1)}, bf16[40,2,128,128]{3,2,1,0:T(8,128)(2,1)}, u32[]{:S(2)}, u32[]{:S(2)}) collective-permute-start(bf16[40,2,128,128]{3,2,1,0:T(8,128)(2,1)} %collective-permute-done.10.refs_13_), channel_id=1, source_target_pairs={{2,4},{4,6},{3,5},{5,7},{10,12},{12,14},{11,13},{13,15},{18,20},{2... | collective-permute-start | bytes 7864328 | tf_op jit(solution)/shard_map/ppermute | solution.py:384
  313.0 38.6 %collective-permute-done.6.refs_2_.refs_3_.refs_1_.refs_17_.refs_16_ = bf16[28,2,128,128]{3,2,1,0:T(8,128)(2,1)S(1)} collective-permute-done((bf16[28,2,128,128]{3,2,1,0:T(8,128)(2,1)}, bf16[28,2,128,128]{3,2,1,0:T(8,128)(2,1)S(1)}, u32[]{:S(2)}, u32[]{:S(2)}) %collective-permute-start.6) | collective-permute-done | bytes 1835040 | tf_op jit(solution)/shard_map/ppermute | solution.py:384
  351.6 2.6 collective-permute-start.5
  354.1 3.6 collective-permute-start.7
  359.1 2.9 pick.5
  362.0 4.5 collective-permute-done.11.refs_9_
  369.4 28.1 %collective-permute-done.5.refs_0_.refs_10_ = bf16[28,2,128,128]{3,2,1,0:T(8,128)(2,1)} collective-permute-done((bf16[28,2,128,128]{3,2,1,0:T(8,128)(2,1)}, bf16[28,2,128,128]{3,2,1,0:T(8,128)(2,1)}, u32[]{:S(2)}, u32[]{:S(2)}) %collective-permute-start.5) | collective-permute-done | bytes 1835040 | tf_op jit(solution)/shard_map/ppermute | solution.py:384
  410.5 2.8 collective-permute-start.19
  413.3 28.1 %collective-permute-done.20.refs_1_ = bf16[28,2,128,128]{3,2,1,0:T(8,128)(2,1)} collective-permute-done((bf16[28,2,128,128]{3,2,1,0:T(8,128)(2,1)}, bf16[28,2,128,128]{3,2,1,0:T(8,128)(2,1)}, u32[]{:S(2)}, u32[]{:S(2)}) %collective-permute-start.20) | collective-permute-done | bytes 1835040 | tf_op jit(solution)/shard_map/ppermute | solution.py:384
  446.8 2.7 pick.4
  449.6 4.4 collective-permute-start.22
  455.3 46.7 %phase.4.refs_19_ = f32[16,1024,256]{2,1,0:T(8,128)} custom-call(s32[9]{0:T(128)S(1)} %pad_add_fusion.2.refs_0_, s32[17]{0:T(128)} %get-tuple-element.125.refs_1_, s32[256]{0:T(256)} %get-tuple-element.126.refs_2_, s32[256]{0:T(256)} %get-tuple-element.127.refs_3_, s32[256]{0:T(256)} %broadcast_add_fusion.3.refs_4_, f32[4104]{0:T(1024)S(1)} %concatenate.22.refs_5_, ...), custom_call_target="tpu_custom_call" | custom-call | flops 17179869184 | bytes 67108864 | tf_op jit(solution)/shard_map/phase/pallas_call | solution.py:266
  504.0 5.2 collective-permute-start.23
  509.2 31.3 %phase.5 = f32[16,1024,256]{2,1,0:T(8,128)} custom-call(s32[9]{0:T(128)S(1)} %pad_add_fusion.2.refs_0_, s32[17]{0:T(128)} %get-tuple-element.120.refs_1_, s32[128]{0:T(128)} %get-tuple-element.121.refs_2_, s32[128]{0:T(128)} %get-tuple-element.122.refs_3_, s32[128]{0:T(128)} %broadcast_add_fusion.5.refs_4_, f32[4104]{0:T(1024)S(1)} %concatenate.22.refs_5_, ...), custom_call_target="tpu_custom_call" | custom-call | flops 8589934592 | bytes 67108864 | tf_op jit(solution)/shard_map/phase/pallas_call | solution.py:266
  540.6 29.7 %conditional.1 = (bf16[2,1024,2048]{2,1,0:T(8,128)(2,1)}) conditional(s32[]{:T(128)} %convert_element_type.51, (s32[9]{0:T(128)S(1)}, s32[17]{0:T(128)S(1)}, s32[128]{0:T(128)S(1)}, s32[128]{0:T(128)S(1)}, s32[128]{0:T(128)S(1)}, /*index=5*/f32[4104]{0:T(1024)S(1)}, bf16[2,1024,2048]{2,1,0:T(8,128)(2,1)}, bf16[2,1024,2048]{2,1,0:T(8,128)(2,1)}, ...), branch_computations={%region_26.27_spmd, %region_27.29_spmd} | conditional | flops 8589934592 | bytes 495007296 | solution.py:455
  540.6 29.5 %phase.3 = bf16[2,1024,2048]{2,1,0:T(8,128)(2,1)} custom-call(s32[9]{0:T(128)S(1)} %get-tuple-element.53.refs_0_, s32[17]{0:T(128)S(1)} %get-tuple-element.66.refs_1_, s32[128]{0:T(128)S(1)} %get-tuple-element.67.refs_2_, s32[128]{0:T(128)S(1)} %get-tuple-element.68.refs_3_, s32[128]{0:T(128)S(1)} %get-tuple-element.69.refs_4_, ...), custom_call_target="tpu_custom_call" | custom-call | flops 8589934592 | bytes 67108864 | tf_op jit(solution)/shard_map/cond/branch_0_fun/phase/pallas_call | solution.py:266
  (160 shorter events, 55.7 us)
Async XLA Ops:
  0.6 26.4 %copy-start = (s32[32,32]{1,0:T(8,128)S(1)}, s32[32,32]{1,0:T(8,128)}, u32[]{:S(2)}) copy-start(s32[32,32]{1,0:T(8,128)} %param.12) | copy-start | bytes 12292
  6.9 20.4 %copy-start.5 = (s32[32,32]{1,0:T(8,128)S(1)}, s32[32,32]{1,0:T(8,128)}, u32[]{:S(2)}) copy-start(s32[32,32]{1,0:T(8,128)} %param.13) | copy-start | bytes 12292
  11.4 203.9 %collective-permute-start.3 = (bf16[28,2,128,128]{3,2,1,0:T(8,128)(2,1)}, bf16[28,2,128,128]{3,2,1,0:T(8,128)(2,1)S(1)}, u32[]{:S(2)}, u32[]{:S(2)}) collective-permute-start(bf16[28,2,128,128]{3,2,1,0:T(8,128)(2,1)} %pack.4.refs_12_), channel_id=1, source_target_pairs={{1,0},{3,2},{5,4},{7,6},{9,8},{11,10},{13,12},{15,14},{17,16},{19,... | collective-permute-start | bytes 5505032 | tf_op jit(solution)/shard_map/ppermute | solution.py:384
  19.9 237.3 %collective-permute-start.17 = (bf16[40,2,128,128]{3,2,1,0:T(8,128)(2,1)}, bf16[40,2,128,128]{3,2,1,0:T(8,128)(2,1)}, u32[]{:S(2)}, u32[]{:S(2)}) collective-permute-start(bf16[40,2,128,128]{3,2,1,0:T(8,128)(2,1)} %pack.6.refs_9_), channel_id=1, source_target_pairs={{2,0},{4,2},{6,4},{3,1},{5,3},{7,5},{10,8},{12,10},{14,12},{11,9},... | collective-permute-start | bytes 7864328 | tf_op jit(solution)/shard_map/ppermute | solution.py:384
  21.8 239.6 %collective-permute-start.10 = (bf16[40,2,128,128]{3,2,1,0:T(8,128)(2,1)}, bf16[40,2,128,128]{3,2,1,0:T(8,128)(2,1)}, u32[]{:S(2)}, u32[]{:S(2)}) collective-permute-start(bf16[40,2,128,128]{3,2,1,0:T(8,128)(2,1)} %pack.6.refs_9_), channel_id=1, source_target_pairs={{0,2},{2,4},{4,6},{1,3},{3,5},{5,7},{8,10},{10,12},{12,14},{9,11},... | collective-permute-start | bytes 7864328 | tf_op jit(solution)/shard_map/ppermute | solution.py:384
  25.7 423.8 %collective-permute-start.8 = (bf16[2,1024,2048]{2,1,0:T(8,128)(2,1)}, bf16[2,1024,2048]{2,1,0:T(8,128)(2,1)}, u32[]{:S(2)}, u32[]{:S(2)}) collective-permute-start(bf16[2,1024,2048]{2,1,0:T(8,128)(2,1)} %refs_6_.3), channel_id=1, source_target_pairs={{0,1},{2,3},{4,5},{6,7},{8,9},{10,11},{12,13},{14,15},{16,17},{18,... | collective-permute-start | bytes 25165832 | tf_op jit(solution)/shard_map/ppermute | solution.py:384
  28.4 181.0 %collective-permute-start.27 = (s32[1]{0:T(128)}, s32[1]{0:T(128)}, u32[]{:S(2)}, u32[]{:S(2)}) collective-permute-start(s32[1]{0:T(128)} %bitcast.34), channel_id=1, source_target_pairs={{0,1},{1,0},{2,3},{3,2},{4,5},{5,4},{6,7},{7,6},{8,9},{9,8},{10,11... | collective-permute-start | bytes 20 | tf_op jit(solution)/shard_map/ppermute | solution.py:384
  209.3 244.7 %collective-permute-start.9 = (bf16[2,1024,2048]{2,1,0:T(8,128)(2,1)}, bf16[2,1024,2048]{2,1,0:T(8,128)(2,1)}, u32[]{:S(2)}, u32[]{:S(2)}) collective-permute-start(bf16[2,1024,2048]{2,1,0:T(8,128)(2,1)} %refs_6_.3), channel_id=1, source_target_pairs={{1,0},{3,2},{5,4},{7,6},{9,8},{11,10},{13,12},{15,14},{17,16},{19,... | collective-permute-start | bytes 25165832 | tf_op jit(solution)/shard_map/ppermute | solution.py:384
  215.3 7.1 %collective-permute-start.28 = (s32[1]{0:T(128)}, s32[1]{0:T(128)}, u32[]{:S(2)}, u32[]{:S(2)}) collective-permute-start(s32[1]{0:T(128)} %add.331), channel_id=1, source_target_pairs={{0,2},{2,4},{4,6},{6,0},{1,3},{3,5},{5,7},{7,1},{8,10},{10,12},{12... | collective-permute-start | bytes 20 | tf_op jit(solution)/shard_map/ppermute | solution.py:384
  222.3 4.5 collective-permute-start.29
  226.8 3.5 collective-permute-start.30
  230.4 11.3 %collective-permute-start.14 = (bf16[8,2,128,128]{3,2,1,0:T(8,128)(2,1)}, bf16[8,2,128,128]{3,2,1,0:T(8,128)(2,1)S(1)}, u32[]{:S(2)}, u32[]{:S(2)}) collective-permute-start(bf16[8,2,128,128]{3,2,1,0:T(8,128)(2,1)} %pack.7.refs_11_), channel_id=1, source_target_pairs={{0,2},{2,4},{4,6},{1,3},{3,5},{5,7},{8,10},{10,12},{12,14},{9,11},... | collective-permute-start | bytes 1572872 | tf_op jit(solution)/shard_map/ppermute | solution.py:384
  241.6 23.8 %copy-start.7 = (bf16[8,2,128,128]{3,2,1,0:T(8,128)(2,1)}, bf16[8,2,128,128]{3,2,1,0:T(8,128)(2,1)S(1)}, u32[]{:S(2)}) copy-start(bf16[8,2,128,128]{3,2,1,0:T(8,128)(2,1)S(1)} %collective-permute-done.14.refs_15_) | copy-start | bytes 1572868
  241.6 11.3 %collective-permute-start.21 = (bf16[8,2,128,128]{3,2,1,0:T(8,128)(2,1)}, bf16[8,2,128,128]{3,2,1,0:T(8,128)(2,1)S(1)}, u32[]{:S(2)}, u32[]{:S(2)}) collective-permute-start(bf16[8,2,128,128]{3,2,1,0:T(8,128)(2,1)} %pack.7.refs_11_), channel_id=1, source_target_pairs={{2,0},{4,2},{6,4},{3,1},{5,3},{7,5},{10,8},{12,10},{14,12},{11,9},... | collective-permute-start | bytes 1572872 | tf_op jit(solution)/shard_map/ppermute | solution.py:384
  252.9 51.6 %collective-permute-start.4 = (bf16[28,2,128,128]{3,2,1,0:T(8,128)(2,1)}, bf16[28,2,128,128]{3,2,1,0:T(8,128)(2,1)}, u32[]{:S(2)}, u32[]{:S(2)}) collective-permute-start(bf16[28,2,128,128]{3,2,1,0:T(8,128)(2,1)} %pack.5.refs_10_), channel_id=1, source_target_pairs={{0,2},{2,4},{4,6},{1,3},{3,5},{5,7},{8,10},{10,12},{12,14},{9,11},... | collective-permute-start | bytes 5505032 | tf_op jit(solution)/shard_map/ppermute | solution.py:384
  257.2 97.0 %collective-permute-start.18 = (bf16[40,2,128,128]{3,2,1,0:T(8,128)(2,1)}, bf16[40,2,128,128]{3,2,1,0:T(8,128)(2,1)}, u32[]{:S(2)}, u32[]{:S(2)}) collective-permute-start(bf16[40,2,128,128]{3,2,1,0:T(8,128)(2,1)} %collective-permute-done.17.refs_16_.refs_15_), channel_id=1, source_target_pairs={{2,0},{4,2},{3,1},{5,3},{10,8},{12,10},{11,9},{13,11},{18,16},{20,... | collective-permute-start | bytes 7864328 | tf_op jit(solution)/shard_map/ppermute | solution.py:384
  261.4 38.8 %collective-permute-start.15 = (bf16[8,2,128,128]{3,2,1,0:T(8,128)(2,1)S(1)}, bf16[8,2,128,128]{3,2,1,0:T(8,128)(2,1)S(1)}, u32[]{:S(2)}, u32[]{:S(2)}) collective-permute-start(bf16[8,2,128,128]{3,2,1,0:T(8,128)(2,1)S(1)} %collective-permute-done.14.refs_15_), channel_id=1, source_target_pairs={{2,4},{4,6},{3,5},{5,7},{10,12},{12,14},{11,13},{13,15},{18,20},{2... | collective-permute-start | bytes 1572872 | tf_op jit(solution)/shard_map/ppermute | solution.py:384
  300.3 149.3 %copy-start.4 = (bf16[8,2,128,128]{3,2,1,0:T(8,128)(2,1)}, bf16[8,2,128,128]{3,2,1,0:T(8,128)(2,1)S(1)}, u32[]{:S(2)}) copy-start(bf16[8,2,128,128]{3,2,1,0:T(8,128)(2,1)S(1)} %collective-permute-done.15.refs_11_) | copy-start | bytes 1572868
  300.3 51.3 %collective-permute-start.6 = (bf16[28,2,128,128]{3,2,1,0:T(8,128)(2,1)}, bf16[28,2,128,128]{3,2,1,0:T(8,128)(2,1)S(1)}, u32[]{:S(2)}, u32[]{:S(2)}) collective-permute-start(bf16[28,2,128,128]{3,2,1,0:T(8,128)(2,1)} %pack.5.refs_10_), channel_id=1, source_target_pairs={{2,0},{4,2},{6,4},{3,1},{5,3},{7,5},{10,8},{12,10},{14,12},{11,9},... | collective-permute-start | bytes 5505032 | tf_op jit(solution)/shard_map/ppermute | solution.py:384
  304.5 61.9 %collective-permute-start.11 = (bf16[40,2,128,128]{3,2,1,0:T(8,128)(2,1)}, bf16[40,2,128,128]{3,2,1,0:T(8,128)(2,1)}, u32[]{:S(2)}, u32[]{:S(2)}) collective-permute-start(bf16[40,2,128,128]{3,2,1,0:T(8,128)(2,1)} %collective-permute-done.10.refs_13_), channel_id=1, source_target_pairs={{2,4},{4,6},{3,5},{5,7},{10,12},{12,14},{11,13},{13,15},{18,20},{2... | collective-permute-start | bytes 7864328 | tf_op jit(solution)/shard_map/ppermute | solution.py:384
  351.6 45.9 %collective-permute-start.5 = (bf16[28,2,128,128]{3,2,1,0:T(8,128)(2,1)}, bf16[28,2,128,128]{3,2,1,0:T(8,128)(2,1)}, u32[]{:S(2)}, u32[]{:S(2)}) collective-permute-start(bf16[28,2,128,128]{3,2,1,0:T(8,128)(2,1)} %collective-permute-done.4.refs_0_.refs_14_), channel_id=1, source_target_pairs={{2,4},{4,6},{3,5},{5,7},{10,12},{12,14},{11,13},{13,15},{18,20},{2... | collective-permute-start | bytes 5505032 | tf_op jit(solution)/shard_map/ppermute | solution.py:384
  354.1 45.3 %collective-permute-start.7 = (bf16[28,2,128,128]{3,2,1,0:T(8,128)(2,1)S(1)}, bf16[28,2,128,128]{3,2,1,0:T(8,128)(2,1)}, u32[]{:S(2)}, u32[]{:S(2)}) collective-permute-start(bf16[28,2,128,128]{3,2,1,0:T(8,128)(2,1)S(1)} %collective-permute-done.6.refs_2_.refs_3_.refs_1_.refs_17_.refs_16_), channel_id=1, source_target_pairs={{2,0},{4,2},{3,1},{5,3},{10,8},{12,10},{11,9},{13,11},{18,16},{20,... | collective-permute-start | bytes 5505032 | tf_op jit(solution)/shard_map/ppermute | solution.py:384
  366.5 42.7 %collective-permute-start.26 = (bf16[28,2,128,128]{3,2,1,0:T(8,128)(2,1)}, bf16[28,2,128,128]{3,2,1,0:T(8,128)(2,1)}, u32[]{:S(2)}, u32[]{:S(2)}) collective-permute-start(bf16[28,2,128,128]{3,2,1,0:T(8,128)(2,1)} %pick.5), channel_id=1, source_target_pairs={{0,1},{2,3},{4,5},{6,7},{8,9},{10,11},{12,13},{14,15},{16,17},{18,... | collective-permute-start | bytes 5505032 | tf_op jit(solution)/shard_map/ppermute | solution.py:384
  397.5 13.0 %collective-permute-start.13 = (bf16[28,2,128,128]{3,2,1,0:T(8,128)(2,1)}, bf16[28,2,128,128]{3,2,1,0:T(8,128)(2,1)}, u32[]{:S(2)}, u32[]{:S(2)}) collective-permute-start(bf16[28,2,128,128]{3,2,1,0:T(8,128)(2,1)} %collective-permute-done.5.refs_0_.refs_10_), channel_id=1, source_target_pairs={{4,6},{5,7},{12,14},{13,15},{20,22},{21,23},{28,30},{29,31}} | collective-permute-start | bytes 5505032 | tf_op jit(solution)/shard_map/ppermute | solution.py:384
  399.4 42.0 %collective-permute-start.20 = (bf16[28,2,128,128]{3,2,1,0:T(8,128)(2,1)}, bf16[28,2,128,128]{3,2,1,0:T(8,128)(2,1)}, u32[]{:S(2)}, u32[]{:S(2)}) collective-permute-start(bf16[28,2,128,128]{3,2,1,0:T(8,128)(2,1)} %collective-permute-done.7.refs_1_.refs_2_.refs_13_), channel_id=1, source_target_pairs={{2,0},{3,1},{10,8},{11,9},{18,16},{19,17},{26,24},{27,25}} | collective-permute-start | bytes 5505032 | tf_op jit(solution)/shard_map/ppermute | solution.py:384
  409.2 94.8 %collective-permute-start.25 = (bf16[28,2,128,128]{3,2,1,0:T(8,128)(2,1)}, bf16[28,2,128,128]{3,2,1,0:T(8,128)(2,1)}, u32[]{:S(2)}, u32[]{:S(2)}) collective-permute-start(bf16[28,2,128,128]{3,2,1,0:T(8,128)(2,1)} %pick.3), channel_id=1, source_target_pairs={{0,1},{2,3},{4,5},{6,7},{8,9},{10,11},{12,13},{14,15},{16,17},{18,... | collective-permute-start | bytes 5505032 | tf_op jit(solution)/shard_map/ppermute | solution.py:384
  410.5 130.1 %collective-permute-start.19 = (bf16[40,2,128,128]{3,2,1,0:T(8,128)(2,1)}, bf16[40,2,128,128]{3,2,1,0:T(8,128)(2,1)}, u32[]{:S(2)}, u32[]{:S(2)}) collective-permute-start(bf16[40,2,128,128]{3,2,1,0:T(8,128)(2,1)} %collective-permute-done.18.refs_12_), channel_id=1, source_target_pairs={{2,0},{3,1},{10,8},{11,9},{18,16},{19,17},{26,24},{27,25}} | collective-permute-start | bytes 7864328 | tf_op jit(solution)/shard_map/ppermute | solution.py:384
  441.4 99.2 %collective-permute-start.12 = (bf16[40,2,128,128]{3,2,1,0:T(8,128)(2,1)}, bf16[40,2,128,128]{3,2,1,0:T(8,128)(2,1)}, u32[]{:S(2)}, u32[]{:S(2)}) collective-permute-start(bf16[40,2,128,128]{3,2,1,0:T(8,128)(2,1)} %collective-permute-done.11.refs_9_), channel_id=1, source_target_pairs={{4,6},{5,7},{12,14},{13,15},{20,22},{21,23},{28,30},{29,31}} | collective-permute-start | bytes 7864328 | tf_op jit(solution)/shard_map/ppermute | solution.py:384
  449.6 53.0 %collective-permute-start.22 = (bf16[8,2,128,128]{3,2,1,0:T(8,128)(2,1)S(1)}, bf16[8,2,128,128]{3,2,1,0:T(8,128)(2,1)S(1)}, u32[]{:S(2)}, u32[]{:S(2)}) collective-permute-start(bf16[8,2,128,128]{3,2,1,0:T(8,128)(2,1)S(1)} %collective-permute-done.21.refs_18_.refs_17_), channel_id=1, source_target_pairs={{2,0},{4,2},{3,1},{5,3},{10,8},{12,10},{11,9},{13,11},{18,16},{20,... | collective-permute-start | bytes 1572872 | tf_op jit(solution)/shard_map/ppermute | solution.py:384
  454.0 86.6 %collective-permute-start.24 = (bf16[28,2,128,128]{3,2,1,0:T(8,128)(2,1)}, bf16[28,2,128,128]{3,2,1,0:T(8,128)(2,1)}, u32[]{:S(2)}, u32[]{:S(2)}) collective-permute-start(bf16[28,2,128,128]{3,2,1,0:T(8,128)(2,1)} %pick.4), channel_id=1, source_target_pairs={{0,1},{2,3},{4,5},{6,7},{8,9},{10,11},{12,13},{14,15},{16,17},{18,... | collective-permute-start | bytes 5505032 | tf_op jit(solution)/shard_map/ppermute | solution.py:384
  502.5 38.0 %collective-permute-start.16 = (bf16[8,2,128,128]{3,2,1,0:T(8,128)(2,1)}, bf16[8,2,128,128]{3,2,1,0:T(8,128)(2,1)}, u32[]{:S(2)}, u32[]{:S(2)}) collective-permute-start(bf16[8,2,128,128]{3,2,1,0:T(8,128)(2,1)} %copy-done.4), channel_id=1, source_target_pairs={{4,6},{5,7},{12,14},{13,15},{20,22},{21,23},{28,30},{29,31}} | collective-permute-start | bytes 1572872 | tf_op jit(solution)/shard_map/ppermute | solution.py:384
  504.0 36.5 %collective-permute-start.23 = (bf16[8,2,128,128]{3,2,1,0:T(8,128)(2,1)S(1)}, bf16[8,2,128,128]{3,2,1,0:T(8,128)(2,1)}, u32[]{:S(2)}, u32[]{:S(2)}) collective-permute-start(bf16[8,2,128,128]{3,2,1,0:T(8,128)(2,1)S(1)} %collective-permute-done.22.refs_14_), channel_id=1, source_target_pairs={{2,0},{3,1},{10,8},{11,9},{18,16},{19,17},{26,24},{27,25}} | collective-permute-start | bytes 1572872 | tf_op jit(solution)/shard_map/ppermute | solution.py:384
  (3 other events, 25.4 us)
